TPU v7x, 32 devices: a whole 2x2x4 slice. The times are simulated.
32 devices in a mesh: parts: 2 (over x), cluster: 16 (over z, y, core).
Axes of the slice: x: 2, y: 2, z: 4, core: 2. Of those that a mesh axis runs over, the one named last changes fastest.
Arguments:
- queries: float32 [4096, 1024], P(('parts', 'cluster')), parts along dimension 0, may hold values from -1 to 1
- passages: float32 [64, 128, 1024], P(('parts', 'cluster')), parts along dimension 0, may hold values from -6 to 6
- first_blocks: int32 [4096, 4], P(('parts', 'cluster')), parts along dimension 0, may hold values from 0 to 31, all different within a row; in each aligned block of 128 rows (0 to 127, 128 to 255, ...) at most 24 rows name the same one
- followup_blocks: int32 [4096, 4], P(('parts', 'cluster')), parts along dimension 0, may hold values from 0 to 31, all different within a row; in each aligned block of 128 rows (0 to 127, 128 to 255, ...) at most 24 rows name the same one
Outputs:
- expanded: float32 [4096, 1024], P(('parts', 'cluster')), parts along dimension 0
- second_scores: float32 [4096, 4, 128], P(('parts', 'cluster')), parts along dimension 0
There are 2 independent parts, one for each index of `parts`. A program takes and returns all parts, laid end to end along the dimension named above; each array names one. Nothing has to cross between parts.
Inputs may be any that keep to these rules, and one draw needn't show every extreme that they name: `first_blocks`: each row names 4 different blocks; among the queries of one device no block is named more than 24 times, and some block is named exactly 24 times. `followup_blocks`: each row names 4 different blocks; among the queries of one device no block is named more than 24 times, and some block is named exactly 24 times.
All inputs are finite; a program needn't handle non-finite values.
Results may differ from a plain program's by a relative error of at most 0.00014.
Values sent between devices are 32-bit elements; how exact they have to be, the bound alone decides.
No kernel may reach another device: no remote copies, remote signals or barrier semaphores. Data moves between devices by JAX's collectives and lax.ppermute only.
A program may use at most 128 MiB of HBM per device.

v0:
```python
import functools

import jax
import jax.numpy as jnp
import numpy as np
from jax import lax
from jax.experimental import pallas as pl
from jax.experimental.pallas import tpu as pltpu
from jax.sharding import PartitionSpec as P


SOFTMAX_HEAT = 2.0
FEEDBACK = 0.5
LOWEST = -3.0e38
NT = (((1,), (1,)), ((), ()))
NN = (((1,), (0,)), ((), ()))


def position_targets(block_ids, capacity):
    flat_ids = block_ids.reshape(-1)
    matches = flat_ids[:, None] == flat_ids[None, :]
    positions = jnp.arange(flat_ids.shape[0], dtype=jnp.int32)
    earlier = positions[None, :] < positions[:, None]
    ranking = jnp.sum(jnp.logical_and(matches, earlier), axis=1, dtype=jnp.int32)
    return flat_ids * capacity + ranking


def pack_rows(values, targets, owners, resident_blocks, capacity):
    buffer = jnp.zeros((owners * resident_blocks * capacity, values.shape[1]), values.dtype)
    buffer = buffer.at[targets].set(values)
    return buffer.reshape(owners, resident_blocks, capacity, values.shape[1])


def reply(results):
    return (
        lax.all_to_all(results[0], "cluster", split_axis=0, concat_axis=0, tiled=True),
        lax.all_to_all(results[1], "cluster", split_axis=0, concat_axis=0, tiled=True),
        lax.all_to_all(results[2], "cluster", split_axis=0, concat_axis=0, tiled=True),
    )


def send_back(match_scores):
    return lax.all_to_all(match_scores, "cluster", split_axis=0, concat_axis=0, tiled=True)


def routed(queries, passages, first_blocks, followup_blocks):
    owners = lax.axis_size("cluster")
    resident_blocks = passages.shape[0]
    embed_width = queries.shape[1]
    per_query = first_blocks.shape[1]
    pair_count = queries.shape[0] * per_query
    all_blocks = owners * resident_blocks
    capacity = max(2, (3 * pair_count + 2 * all_blocks - 1) // (2 * all_blocks))
    coefficient = FEEDBACK * embed_width ** (-0.5)
    highest = lax.Precision.HIGHEST

    def project_onto_centroid(arrived):
        return jnp.einsum("nbce,bre->nbcr", arrived, passages, precision=highest)

    first_targets = position_targets(first_blocks, capacity)
    second_targets = position_targets(followup_blocks, capacity)
    repeated = jnp.repeat(queries, per_query, axis=0)
    first_sent = pack_rows(repeated, first_targets, owners, resident_blocks, capacity)
    match_scores = SOFTMAX_HEAT * project_onto_centroid(
        lax.all_to_all(first_sent, "cluster", split_axis=0, concat_axis=0, tiled=True)
    )
    highs = jnp.max(match_scores, axis=3)
    weights = jnp.exp(match_scores - highs[..., None])
    totals = jnp.sum(weights, axis=3)
    vectors = jnp.einsum("nbcr,bre->nbce", weights, passages, precision=highest)
    highs, totals, vectors = reply((highs, totals, vectors))
    highs = highs.reshape(-1)[first_targets].reshape(-1, per_query)
    totals = totals.reshape(-1)[first_targets].reshape(-1, per_query)
    vectors = vectors.reshape(-1, embed_width)[first_targets].reshape(-1, per_query, embed_width)
    peak_high = jnp.max(highs, axis=1, keepdims=True)
    scaled = jnp.exp(highs - peak_high)
    denominator = jnp.sum(scaled * totals, axis=1)
    feedback = jnp.einsum("qk,qke->qe", scaled, vectors, precision=highest) / denominator[:, None]
    expanded = queries + coefficient * feedback
    expanded_sent = pack_rows(
        jnp.repeat(expanded, per_query, axis=0), second_targets, owners, resident_blocks, capacity
    )
    returned = (lambda arrived: send_back(project_onto_centroid(arrived)))(
        lax.all_to_all(expanded_sent, "cluster", split_axis=0, concat_axis=0, tiled=True)
    )
    second_scores = returned.reshape(-1, returned.shape[3])[second_targets].reshape(
        queries.shape[0], per_query, -1
    )
    return (expanded, second_scores)


class Ladder:
    def __init__(self, where):
        self.where = where
        self.spot = {place: i for i, place in enumerate(where)}

    def hop(self, pairs):
        return [
            (self.spot[a, y, c], self.spot[b, y, c]) for a, b in pairs for y in (0, 1) for c in (0, 1)
        ]

    def across(self, levels=(0, 1, 2, 3)):
        return [
            (i, self.spot[z, 1 - y, c]) for i, (z, y, c) in enumerate(self.where) if z in levels
        ]

    def sibling(self):
        return [(i, self.spot[z, y, 1 - c]) for i, (z, y, c) in enumerate(self.where)]


def ladder_of(mesh):
    groups = np.moveaxis(mesh.devices, mesh.axis_names.index("cluster"), -1)
    groups = groups.reshape(-1, groups.shape[-1])
    found = []
    for group in groups:
        if not all(hasattr(d, "coords") and hasattr(d, "core_on_chip") for d in group):
            return None
        spots = np.array([[*d.coords, d.core_on_chip] for d in group])
        kinds = [np.unique(column) for column in spots.T]
        order = sorted(range(3), key=lambda k: -len(kinds[k]))
        if [len(kinds[k]) for k in order] != [4, 2, 1] or len(kinds[3]) != 2:
            return None
        use = (order[0], order[1], 3)
        found.append([tuple(int(np.searchsorted(kinds[k], s[k])) for k in use) for s in spots])
    if any(f != found[0] for f in found) or len(set(found[0])) != len(found[0]):
        return None
    return Ladder(found[0])


def split(x):
    high = x.astype(jnp.bfloat16)
    return high, (x - high.astype(jnp.float32)).astype(jnp.bfloat16)


def dot(a, b, dims):
    return lax.dot_general(a, b, dims, preferred_element_type=jnp.float32)


def three_way(stacked, high, low, dims):
    rows = stacked.shape[0] // 2
    both = dot(stacked, high, dims)
    return both[:rows] + both[rows:] + dot(stacked[:rows], low, dims)


def stacked_halves(x):
    high, low = split(x)
    return jnp.concatenate([high, low], axis=0)


def first_round(ids, base, slots, inner, queries, named, state, high_ref, low_ref, score_ref):
    rows = slots[0][0].shape[0]
    count = len(slots)
    for k, refs in enumerate(slots):
        block = refs[0][...]
        if len(refs) == 2:
            block = jnp.where(inner, block, refs[1][...])
        high, low = split(block)
        high_ref[k * rows : (k + 1) * rows, :] = high
        low_ref[k * rows : (k + 1) * rows, :] = low
    asked = stacked_halves(queries)
    scores = SOFTMAX_HEAT * three_way(asked, high_ref[...], low_ref[...], NT)
    top = None
    for k in range(count):
        mine = named[0] == ids[base + k]
        for column in named[1:]:
            mine = jnp.logical_or(mine, column == ids[base + k])
        part = jnp.where(mine, scores[:, k * rows : (k + 1) * rows], LOWEST)
        score_ref[:, k * rows : (k + 1) * rows] = part
        top = part if top is None else jnp.maximum(top, part)
    peak, total, vector = state
    new_peak = jnp.maximum(peak, jnp.max(top, axis=1, keepdims=True))
    held = score_ref[...]
    weights = jnp.where(held > LOWEST, jnp.exp(held - new_peak), 0.0)
    scale = jnp.exp(peak - new_peak)
    total = scale * total + jnp.sum(weights, axis=1, keepdims=True)
    gained = three_way(stacked_halves(weights), high_ref[...], low_ref[...], NN)
    return new_peak, total, scale * vector + gained


def columns_of(ref, width):
    return [
        jnp.broadcast_to(ref[:, j : j + 1], (ref.shape[0], width)) for j in range(ref.shape[1])
    ]


def step_kernel(shape, base, fresh, ids, *refs):
    at = 0
    slots = []
    for n in shape:
        slots.append(refs[at : at + n])
        at += n
    q_ref, fb_ref = refs[at : at + 2]
    at += 2
    rows = slots[0][0].shape[0]
    if fresh:
        state = (
            jnp.full((q_ref.shape[0], 1), LOWEST, jnp.float32),
            jnp.zeros((q_ref.shape[0], 1), jnp.float32),
            jnp.zeros(q_ref.shape, jnp.float32),
        )
    else:
        stat, vec = refs[at : at + 2]
        at += 2
        state = (stat[:, 0:1], stat[:, 1:2], vec[...])
    stat_out, vec_out, high_ref, low_ref, score_ref = refs[at:]
    peak, total, vector = first_round(
        ids, base, slots, ids[ids.shape[0] - 1] == 1, q_ref[...], columns_of(fb_ref, rows), state,
        high_ref, low_ref, score_ref,
    )
    lane = lax.broadcasted_iota(jnp.int32, stat_out.shape, 1)
    stat_out[...] = jnp.where(lane == 0, peak, total)
    vec_out[...] = vector


def last_kernel(shape, base, held, coefficient, ids, *refs):
    at = 0
    slots = []
    for n in shape:
        slots.append(refs[at : at + n])
        at += n
    q_ref, fb_ref, ub_ref, stat, vec = refs[at : at + 5]
    at += 5
    kept = []
    for start, count in held:
        kept.append((start, count, refs[at], refs[at + 1]))
        at += 2
    expanded_ref, second_ref, high_ref, low_ref, score_ref, named_ref = refs[at:]
    rows = slots[0][0].shape[0]
    kept.append((base, len(shape), high_ref, low_ref))
    queries = q_ref[...]
    _, total, vector = first_round(
        ids, base, slots, ids[ids.shape[0] - 1] == 1, queries, columns_of(fb_ref, rows),
        (stat[:, 0:1], stat[:, 1:2], vec[...]), high_ref, low_ref, score_ref,
    )
    expanded = queries + coefficient * (vector / total)
    expanded_ref[...] = expanded
    asked = stacked_halves(expanded)
    per_query = ub_ref.shape[1]
    for j in range(per_query):
        named_ref[j] = jnp.broadcast_to(ub_ref[:, j : j + 1], (ub_ref.shape[0], rows))
    picked = [jnp.zeros((queries.shape[0], rows), jnp.float32) for _ in range(per_query)]
    for start, count, high, low in kept:
        scores = three_way(asked, high[...], low[...], NT)
        for k in range(count):
            part = scores[:, k * rows : (k + 1) * rows]
            for j in range(per_query):
                picked[j] = jnp.where(named_ref[j] == ids[start + k], part, picked[j])
    for j in range(per_query):
        second_ref[:, j, :] = picked[j]


VMEM = pl.BlockSpec(memory_space=pltpu.VMEM)
SMEM = pl.BlockSpec(memory_space=pltpu.SMEM)


def cost(queries, count, block, rounds):
    flops = 2 * 3 * queries.shape[0] * count * block.shape[0] * block.shape[1] * rounds
    return pl.CostEstimate(
        flops=flops, transcendentals=queries.shape[0] * count * block.shape[0],
        bytes_accessed=4 * count * block.shape[0] * block.shape[1],
    )


def step_call(slots, base, ids, queries, first_blocks, state):
    block = slots[0][0]
    count, rows, width = len(slots), block.shape[0], block.shape[1]
    flat = [ref for slot in slots for ref in slot]
    extra = [] if state is None else list(state)
    many = queries.shape[0]
    return pl.pallas_call(
        functools.partial(step_kernel, tuple(len(s) for s in slots), base, state is None),
        out_shape=(
            jax.ShapeDtypeStruct((many, rows), jnp.float32),
            jax.ShapeDtypeStruct((many, width), jnp.float32),
            jax.ShapeDtypeStruct((count * rows, width), jnp.bfloat16),
            jax.ShapeDtypeStruct((count * rows, width), jnp.bfloat16),
        ),
        in_specs=[SMEM] + [VMEM] * (len(flat) + 2 + len(extra)),
        out_specs=(VMEM,) * 4,
        scratch_shapes=[pltpu.VMEM((many, count * rows), jnp.float32)],
        compiler_params=pltpu.CompilerParams(vmem_limit_bytes=STEP_VMEM),
        cost_estimate=cost(queries, count, block, 2),
        name="first_round_step",
    )(ids, *flat, queries, first_blocks, *extra)


def last_call(slots, base, ids, queries, first_blocks, followup_blocks, state, held):
    block = slots[0][0]
    count, rows, width = len(slots), block.shape[0], block.shape[1]
    flat = [ref for slot in slots for ref in slot]
    many, per_query = followup_blocks.shape
    kept = [a for _, _, high, low in held for a in (high, low)]
    total = count + sum(n for _, n, _, _ in held)
    return pl.pallas_call(
        functools.partial(
            last_kernel, tuple(len(s) for s in slots), base, tuple((s, n) for s, n, _, _ in held),
            FEEDBACK * width ** (-0.5),
        ),
        out_shape=(
            jax.ShapeDtypeStruct((many, width), jnp.float32),
            jax.ShapeDtypeStruct((many, per_query, rows), jnp.float32),
        ),
        in_specs=[SMEM] + [VMEM] * (len(flat) + 5 + len(kept)),
        out_specs=(VMEM,) * 2,
        scratch_shapes=[
            pltpu.VMEM((count * rows, width), jnp.bfloat16),
            pltpu.VMEM((count * rows, width), jnp.bfloat16),
            pltpu.VMEM((many, count * rows), jnp.float32),
            pltpu.VMEM((per_query, many, rows), jnp.int32),
        ],
        compiler_params=pltpu.CompilerParams(vmem_limit_bytes=LAST_VMEM),
        cost_estimate=cost(queries, total, block, 1),
        name="second_round",
    )(ids, *flat, queries, first_blocks, followup_blocks, *state, *kept)


STEP_VMEM = 12 * 2**20
LAST_VMEM = 12 * 2**20


def slot_owner(slot, z, y):
    inner = z in (1, 2)
    other = 1 - y
    return {
        "own": (z, y), "a1": (z ^ 1, y), "a2": (z ^ 2, y), "a3": (z ^ 3, y),
        "y0": (z, other), "y1": (z ^ 3 if inner else z ^ 1, other), "y2": (z ^ 2, other),
        "y3": (z ^ 1 if inner else z ^ 3, other),
    }[slot]


STAGES = (("own", "a1", "y0"), ("a2", "y1"), ("a3", "y2"), ("y3",))


def gathered(ladder, queries, passages, first_blocks, followup_blocks):
    resident = passages.shape[0]

    def send(x, pairs):
        return lax.ppermute(x, "cluster", pairs)

    full = ladder.hop([(0, 1), (1, 0), (2, 3), (3, 2)])
    middle = ladder.hop([(1, 2), (2, 1)])
    outward = ladder.hop([(1, 0), (2, 3)])
    inward = ladder.hop([(0, 1), (3, 2)])
    across, across_ends = ladder.across(), ladder.across((0, 3))
    sibling = ladder.sibling()

    table = []
    for z, y, c in ladder.where:
        line = []
        for stage in STAGES:
            for slot in stage:
                for core in (c, 1 - c):
                    owner = ladder.spot[(*slot_owner(slot, z, y), core)]
                    line += [owner * resident + r for r in range(resident)]
        table.append(line + [int(z in (1, 2))])
    me = lax.axis_index("cluster")
    ids = lax.dynamic_slice_in_dim(jnp.asarray(np.array(table, np.int32)), me, 1, 0)[0]
    inner = ids[-1] == 1

    pieces = []
    for r in range(resident):
        own = passages[r]
        a1 = send(own, full)
        b1 = send(own, middle)
        y0 = send(own, across)
        a2 = jnp.where(inner, send(a1, middle), send(b1, outward))
        a3 = send(a2, outward)
        y1 = send(jnp.where(inner, b1, a1), across)
        d1 = send(y0, inward)
        y2 = send(a2, across)
        last = send(a3, across_ends) if r % 2 == 0 else send(y2, outward)
        pieces.append({
            "own": (own,), "a1": (a1,), "y0": (y0,), "a2": (a2,), "y1": (y1,), "a3": (b1, a3),
            "y2": (y2,), "y3": (d1, last),
        })
    state, held, base = None, [], 0
    for number, stage in enumerate(STAGES):
        slots = []
        for slot in stage:
            slots += [p[slot] for p in pieces]
            slots += [tuple(send(a, sibling) for a in p[slot]) for p in pieces]
        if number + 1 < len(STAGES):
            stat, vector, high, low = step_call(slots, base, ids, queries, first_blocks, state)
            state = (stat, vector)
            held.append((base, len(slots), high, low))
            base += len(slots)
    return last_call(slots, base, ids, queries, first_blocks, followup_blocks, state, held)


def solution(mesh):
    ladder = ladder_of(mesh)

    def local(queries, passages, first_blocks, followup_blocks):
        owners, resident, rows = lax.axis_size("cluster"), *passages.shape[:2]
        pairs, blocks = first_blocks.size, owners * resident
        capacity = max(2, (3 * pairs + 2 * blocks - 1) // (2 * blocks))
        if ladder is not None and blocks * rows <= 2 * 3 * blocks * capacity:
            return gathered(ladder, queries, passages, first_blocks, followup_blocks)
        return routed(queries, passages, first_blocks, followup_blocks)

    return jax.shard_map(
        local,
        mesh=mesh,
        in_specs=(
            P(("parts", "cluster"), None),
            P(("parts", "cluster"), None, None),
            P(("parts", "cluster"), None),
            P(("parts", "cluster"), None),
        ),
        out_specs=(P(("parts", "cluster"), None), P(("parts", "cluster"), None, None)),
        check_vma=False,
    )
```

profile of v0, /device:TPU:0, one launch (start us, length us, event | category | flops | bytes accessed | tf_op | source)
XLA Modules:
  0.0 181.4 jit_solution(12239465356742571412)
XLA Ops:
  1.9 3.1 %collective-permute-start.2 = (f32[128,1024]{1,0:T(8,128)S(1)}, f32[128,1024]{1,0:T(8,128)S(1)}, u32[]{:S(2)}, u32[]{:S(2)}) collective-permute-start(f32[128,1024]{1,0:T(8,128)S(1)} %get-tuple-element.27.refs_0_), channel_id=1, source_target_pairs={{0,4},{1,5},{2,6},{3,7},{4,0},{5,1},{6,2},{7,3},{8,12},{9,13},{10,... | collective-permute-start | bytes 1572872 | tf_op jit(solution)/shard_map/ppermute | solution.py:338
  5.1 1.9 %collective-permute-start = (f32[128,1024]{1,0:T(8,128)S(1)}, f32[128,1024]{1,0:T(8,128)}, u32[]{:S(2)}, u32[]{:S(2)}) collective-permute-start(f32[128,1024]{1,0:T(8,128)S(1)} %get-tuple-element.27.refs_0_), channel_id=1, source_target_pairs={{0,2},{1,3},{2,0},{3,1},{4,6},{5,7},{6,4},{7,5},{8,10},{9,11},{10,... | collective-permute-start | bytes 1572872 | tf_op jit(solution)/shard_map/ppermute | solution.py:338
  7.1 10.7 %collective-permute-done.2.refs_4_ = f32[128,1024]{1,0:T(8,128)S(1)} collective-permute-done((f32[128,1024]{1,0:T(8,128)S(1)}, f32[128,1024]{1,0:T(8,128)S(1)}, u32[]{:S(2)}, u32[]{:S(2)}) %collective-permute-start.2) | collective-permute-done | bytes 524320 | tf_op jit(solution)/shard_map/ppermute | solution.py:338
  17.8 10.4 %collective-permute-done.10.refs_5_ = f32[128,1024]{1,0:T(8,128)S(1)} collective-permute-done((f32[128,1024]{1,0:T(8,128)S(1)}, f32[128,1024]{1,0:T(8,128)S(1)}, u32[]{:S(2)}, u32[]{:S(2)}) %collective-permute-start.10) | collective-permute-done | bytes 524320 | tf_op jit(solution)/shard_map/ppermute | solution.py:338
  38.7 1.4 collective-permute-start.13
  41.1 1.7 collective-permute-start.30
  43.1 32.4 %collective-permute-done.5 = f32[128,1024]{1,0:T(8,128)S(1)} collective-permute-done((f32[128,1024]{1,0:T(8,128)S(1)}, f32[128,1024]{1,0:T(8,128)S(1)}, u32[]{:S(2)}, u32[]{:S(2)}) %collective-permute-start.5) | collective-permute-done | bytes 524320 | tf_op jit(solution)/shard_map/ppermute | solution.py:338
  76.1 10.4 %collective-permute-done.13 = f32[128,1024]{1,0:T(8,128)S(1)} collective-permute-done((f32[128,1024]{1,0:T(8,128)S(1)}, f32[128,1024]{1,0:T(8,128)S(1)}, u32[]{:S(2)}, u32[]{:S(2)}) %collective-permute-start.13) | collective-permute-done | bytes 524320 | tf_op jit(solution)/shard_map/ppermute | solution.py:338
  86.5 1.5 collective-permute-start.1
  88.1 1.3 collective-permute-start.9
  91.7 8.9 %collective-permute-done.1.refs_0_ = f32[128,1024]{1,0:T(8,128)S(1)} collective-permute-done((f32[128,1024]{1,0:T(8,128)}, f32[128,1024]{1,0:T(8,128)S(1)}, u32[]{:S(2)}, u32[]{:S(2)}) %collective-permute-start.1) | collective-permute-done | bytes 524320 | tf_op jit(solution)/shard_map/ppermute | solution.py:338
  101.9 8.9 %collective-permute-done.9.refs_2_ = f32[128,1024]{1,0:T(8,128)S(1)} collective-permute-done((f32[128,1024]{1,0:T(8,128)S(1)}, f32[128,1024]{1,0:T(8,128)S(1)}, u32[]{:S(2)}, u32[]{:S(2)}) %collective-permute-start.9) | collective-permute-done | bytes 524320 | tf_op jit(solution)/shard_map/ppermute | solution.py:338
  110.8 1.5 collective-permute-start.14
  118.4 7.3 %collective-permute-done.14.refs_9_ = f32[128,1024]{1,0:T(8,128)} collective-permute-done((f32[128,1024]{1,0:T(8,128)S(1)}, f32[128,1024]{1,0:T(8,128)}, u32[]{:S(2)}, u32[]{:S(2)}) %collective-permute-start.14) | collective-permute-done | bytes 524320 | tf_op jit(solution)/shard_map/ppermute | solution.py:338
  125.7 2.2 %collective-permute-done.20.refs_3_ = f32[128,1024]{1,0:T(8,128)} collective-permute-done((f32[128,1024]{1,0:T(8,128)S(1)}, f32[128,1024]{1,0:T(8,128)}, u32[]{:S(2)}, u32[]{:S(2)}) %collective-permute-start.20) | collective-permute-done | bytes 524320 | tf_op jit(solution)/shard_map/ppermute | solution.py:338
  128.7 2.4 %collective-permute-start.7 = (f32[128,1024]{1,0:T(8,128)}, f32[128,1024]{1,0:T(8,128)}, u32[]{:S(2)}, u32[]{:S(2)}) collective-permute-start(f32[128,1024]{1,0:T(8,128)} %collective-permute-done.6.refs_1_), channel_id=1, source_target_pairs={{0,2},{1,3},{2,0},{3,1},{12,14},{13,15},{14,12},{15,13},{16,18},{1... | collective-permute-start | bytes 1572872 | tf_op jit(solution)/shard_map/ppermute | solution.py:338
  131.1 5.1 %collective-permute-done.25.refs_8_ = f32[128,1024]{1,0:T(8,128)} collective-permute-done((f32[128,1024]{1,0:T(8,128)S(1)}, f32[128,1024]{1,0:T(8,128)}, u32[]{:S(2)}, u32[]{:S(2)}) %collective-permute-start.25) | collective-permute-done | bytes 524320 | tf_op jit(solution)/shard_map/ppermute | solution.py:338
  136.2 1.5 collective-permute-start.15
  139.4 6.9 %collective-permute-done.7.refs_1_ = f32[128,1024]{1,0:T(8,128)} collective-permute-done((f32[128,1024]{1,0:T(8,128)}, f32[128,1024]{1,0:T(8,128)}, u32[]{:S(2)}, u32[]{:S(2)}) %collective-permute-start.7) | collective-permute-done | bytes 524320 | tf_op jit(solution)/shard_map/ppermute | solution.py:338
  146.3 3.2 %collective-permute-done.15.refs_3_ = f32[128,1024]{1,0:T(8,128)} collective-permute-done((f32[128,1024]{1,0:T(8,128)}, f32[128,1024]{1,0:T(8,128)}, u32[]{:S(2)}, u32[]{:S(2)}) %collective-permute-start.15) | collective-permute-done | bytes 524320 | tf_op jit(solution)/shard_map/ppermute | solution.py:338
  157.9 5.9 %first_round_step.3 = (f32[128,128]{1,0:T(8,128)S(1)}, f32[128,1024]{1,0:T(8,128)S(1)}, bf16[1536,1024]{1,0:T(8,128)(2,1)S(1)}, bf16[1536,1024]{1,0:T(8,128)(2,1)S(1)}) custom-call(s32[33]{0:T(128)S(1)} %get-tuple-element.29.ids, f32[128,1024]{1,0:T(8,128)S(1)} %copy-done.16, f32[128,1024]{1,0:T(8,128)S(1)} %copy-done.14, f32[128,1024]{1,0:T(8,128)S(1)} %copy-done.21, ...), custom_call_target="tpu_custom_call" | custom-call | flops 2415919104 | bytes 6291456 | tf_op jit(solution)/shard_map/first_round_step/pallas_call | solution.py:270
  164.0 3.5 %first_round_step.4 = (f32[128,128]{1,0:T(8,128)S(1)}, f32[128,1024]{1,0:T(8,128)S(1)}, bf16[1024,1024]{1,0:T(8,128)(2,1)S(1)}, bf16[1024,1024]{1,0:T(8,128)(2,1)S(1)}) custom-call(s32[33]{0:T(128)S(1)} %get-tuple-element.29.ids, f32[128,1024]{1,0:T(8,128)S(1)} %copy-done.10, f32[128,1024]{1,0:T(8,128)S(1)} %copy-done.12, f32[128,1024]{1,0:T(8,128)S(1)} %copy-done.31, ...), custom_call_target="tpu_custom_call" | custom-call | flops 1610612736 | bytes 4194304 | tf_op jit(solution)/shard_map/first_round_step/pallas_call | solution.py:270
  167.5 5.0 %first_round_step.5 = (f32[128,128]{1,0:T(8,128)S(1)}, f32[128,1024]{1,0:T(8,128)S(1)}, bf16[1024,1024]{1,0:T(8,128)(2,1)S(1)}, bf16[1024,1024]{1,0:T(8,128)(2,1)S(1)}) custom-call(s32[33]{0:T(128)S(1)} %get-tuple-element.29.ids, f32[128,1024]{1,0:T(8,128)S(1)} %collective-permute-done.4.refs_0_, f32[128,1024]{1,0:T(8,128)} %collective-permute-done.6.refs_1_, ...), custom_call_target="tpu_custom_call" | custom-call | flops 1610612736 | bytes 4194304 | tf_op jit(solution)/shard_map/first_round_step/pallas_call | solution.py:270
  172.5 8.9 %second_round.1 = (f32[128,1024]{1,0:T(8,128)}, f32[128,4,128]{2,1,0:T(4,128)}) custom-call(s32[33]{0:T(128)S(1)} %get-tuple-element.29.ids, f32[128,1024]{1,0:T(8,128)S(1)} %collective-permute-done.1.refs_0_, f32[128,1024]{1,0:T(8,128)} %collective-permute-done.7.refs_1_, f32[128,1024]{1,0:T(8,128)S(1)} %collective-permute-done.9.refs_2_, ...), custom_call_target="tpu_custom_call" | custom-call | flops 3221225472 | bytes 16777216 | tf_op jit(solution)/shard_map/second_round/pallas_call | solution.py:294
  (149 shorter events, 33.6 us)
Async XLA Ops:
  1.9 15.9 %collective-permute-start.2 = (f32[128,1024]{1,0:T(8,128)S(1)}, f32[128,1024]{1,0:T(8,128)S(1)}, u32[]{:S(2)}, u32[]{:S(2)}) collective-permute-start(f32[128,1024]{1,0:T(8,128)S(1)} %get-tuple-element.27.refs_0_), channel_id=1, source_target_pairs={{0,4},{1,5},{2,6},{3,7},{4,0},{5,1},{6,2},{7,3},{8,12},{9,13},{10,... | collective-permute-start | bytes 1572872 | tf_op jit(solution)/shard_map/ppermute | solution.py:338
  5.0 23.2 %collective-permute-start.10 = (f32[128,1024]{1,0:T(8,128)S(1)}, f32[128,1024]{1,0:T(8,128)S(1)}, u32[]{:S(2)}, u32[]{:S(2)}) collective-permute-start(f32[128,1024]{1,0:T(8,128)S(1)} %get-tuple-element.26.refs_1_), channel_id=1, source_target_pairs={{0,4},{1,5},{2,6},{3,7},{4,0},{5,1},{6,2},{7,3},{8,12},{9,13},{10,... | collective-permute-start | bytes 1572872 | tf_op jit(solution)/shard_map/ppermute | solution.py:338
  5.1 24.6 %collective-permute-start = (f32[128,1024]{1,0:T(8,128)S(1)}, f32[128,1024]{1,0:T(8,128)}, u32[]{:S(2)}, u32[]{:S(2)}) collective-permute-start(f32[128,1024]{1,0:T(8,128)S(1)} %get-tuple-element.27.refs_0_), channel_id=1, source_target_pairs={{0,2},{1,3},{2,0},{3,1},{4,6},{5,7},{6,4},{7,5},{8,10},{9,11},{10,... | collective-permute-start | bytes 1572872 | tf_op jit(solution)/shard_map/ppermute | solution.py:338
  7.0 24.2 %collective-permute-start.8 = (f32[128,1024]{1,0:T(8,128)S(1)}, f32[128,1024]{1,0:T(8,128)S(1)}, u32[]{:S(2)}, u32[]{:S(2)}) collective-permute-start(f32[128,1024]{1,0:T(8,128)S(1)} %get-tuple-element.26.refs_1_), channel_id=1, source_target_pairs={{0,2},{1,3},{2,0},{3,1},{4,6},{5,7},{6,4},{7,5},{8,10},{9,11},{10,... | collective-permute-start | bytes 1572872 | tf_op jit(solution)/shard_map/ppermute | solution.py:338
  7.1 24.1 %collective-permute-start.34 = (f32[128,1024]{1,0:T(8,128)S(1)}, f32[128,1024]{1,0:T(8,128)S(1)}, u32[]{:S(2)}, u32[]{:S(2)}) collective-permute-start(f32[128,1024]{1,0:T(8,128)S(1)} %get-tuple-element.27.refs_0_), channel_id=1, source_target_pairs={{0,1},{1,0},{2,3},{3,2},{4,5},{5,4},{6,7},{7,6},{8,9},{9,8},{10,11... | collective-permute-start | bytes 1572872 | tf_op jit(solution)/shard_map/ppermute | solution.py:338
  36.1 39.4 %collective-permute-start.11 = (f32[128,1024]{1,0:T(8,128)S(1)}, f32[128,1024]{1,0:T(8,128)S(1)}, u32[]{:S(2)}, u32[]{:S(2)}) collective-permute-start(f32[128,1024]{1,0:T(8,128)S(1)} %collective-permute-done.10.refs_5_), channel_id=1, source_target_pairs={{4,8},{5,9},{6,10},{7,11},{8,4},{9,5},{10,6},{11,7},{20,24},{21,25... | collective-permute-start | bytes 1572872 | tf_op jit(solution)/shard_map/ppermute | solution.py:338
  37.3 38.2 %collective-permute-start.5 = (f32[128,1024]{1,0:T(8,128)S(1)}, f32[128,1024]{1,0:T(8,128)S(1)}, u32[]{:S(2)}, u32[]{:S(2)}) collective-permute-start(f32[128,1024]{1,0:T(8,128)S(1)} %collective-permute-done.4.refs_0_), channel_id=1, source_target_pairs={{4,0},{5,1},{6,2},{7,3},{8,12},{9,13},{10,14},{11,15},{20,16},{21,... | collective-permute-start | bytes 1572872 | tf_op jit(solution)/shard_map/ppermute | solution.py:338
  38.7 47.8 %collective-permute-start.13 = (f32[128,1024]{1,0:T(8,128)S(1)}, f32[128,1024]{1,0:T(8,128)S(1)}, u32[]{:S(2)}, u32[]{:S(2)}) collective-permute-start(f32[128,1024]{1,0:T(8,128)S(1)} %collective-permute-done.12.refs_2_), channel_id=1, source_target_pairs={{4,0},{5,1},{6,2},{7,3},{8,12},{9,13},{10,14},{11,15},{20,16},{21,... | collective-permute-start | bytes 1572872 | tf_op jit(solution)/shard_map/ppermute | solution.py:338
  41.1 47.0 %collective-permute-start.30 = (f32[128,1024]{1,0:T(8,128)S(1)}, f32[128,1024]{1,0:T(8,128)S(1)}, u32[]{:S(2)}, u32[]{:S(2)}) collective-permute-start(f32[128,1024]{1,0:T(8,128)S(1)} %broadcast_select_fusion.1), channel_id=1, source_target_pairs={{0,2},{1,3},{2,0},{3,1},{4,6},{5,7},{6,4},{7,5},{8,10},{9,11},{10,... | collective-permute-start | bytes 1572872 | tf_op jit(solution)/shard_map/ppermute | solution.py:338
  42.7 46.7 %collective-permute-start.31 = (f32[128,1024]{1,0:T(8,128)S(1)}, f32[128,1024]{1,0:T(8,128)S(1)}, u32[]{:S(2)}, u32[]{:S(2)}) collective-permute-start(f32[128,1024]{1,0:T(8,128)S(1)} %broadcast_select_fusion), channel_id=1, source_target_pairs={{0,2},{1,3},{2,0},{3,1},{4,6},{5,7},{6,4},{7,5},{8,10},{9,11},{10,... | collective-permute-start | bytes 1572872 | tf_op jit(solution)/shard_map/ppermute | solution.py:338
  88.1 22.7 %collective-permute-start.9 = (f32[128,1024]{1,0:T(8,128)S(1)}, f32[128,1024]{1,0:T(8,128)S(1)}, u32[]{:S(2)}, u32[]{:S(2)}) collective-permute-start(f32[128,1024]{1,0:T(8,128)S(1)} %copy-done.18), channel_id=1, source_target_pairs={{0,4},{1,5},{2,6},{3,7},{12,8},{13,9},{14,10},{15,11},{16,20},{17,... | collective-permute-start | bytes 1572872 | tf_op jit(solution)/shard_map/ppermute | solution.py:338
  89.4 22.9 %collective-permute-start.28 = (f32[128,1024]{1,0:T(8,128)S(1)}, f32[128,1024]{1,0:T(8,128)S(1)}, u32[]{:S(2)}, u32[]{:S(2)}) collective-permute-start(f32[128,1024]{1,0:T(8,128)S(1)} %broadcast_select_fusion.3.refs_0_), channel_id=1, source_target_pairs={{0,1},{1,0},{2,3},{3,2},{4,5},{5,4},{6,7},{7,6},{8,9},{9,8},{10,11... | collective-permute-start | bytes 1572872 | tf_op jit(solution)/shard_map/ppermute | solution.py:338
  89.5 25.6 %collective-permute-start.29 = (f32[128,1024]{1,0:T(8,128)S(1)}, f32[128,1024]{1,0:T(8,128)S(1)}, u32[]{:S(2)}, u32[]{:S(2)}) collective-permute-start(f32[128,1024]{1,0:T(8,128)S(1)} %broadcast_select_fusion.2.refs_1_), channel_id=1, source_target_pairs={{0,1},{1,0},{2,3},{3,2},{4,5},{5,4},{6,7},{7,6},{8,9},{9,8},{10,11... | collective-permute-start | bytes 1572872 | tf_op jit(solution)/shard_map/ppermute | solution.py:338
  90.8 26.0 %collective-permute-start.32 = (f32[128,1024]{1,0:T(8,128)S(1)}, f32[128,1024]{1,0:T(8,128)S(1)}, u32[]{:S(2)}, u32[]{:S(2)}) collective-permute-start(f32[128,1024]{1,0:T(8,128)S(1)} %collective-permute-done.30.refs_4_), channel_id=1, source_target_pairs={{0,1},{1,0},{2,3},{3,2},{4,5},{5,4},{6,7},{7,6},{8,9},{9,8},{10,11... | collective-permute-start | bytes 1572872 | tf_op jit(solution)/shard_map/ppermute | solution.py:338
  100.6 17.6 %collective-permute-start.6 = (f32[128,1024]{1,0:T(8,128)S(1)}, f32[128,1024]{1,0:T(8,128)}, u32[]{:S(2)}, u32[]{:S(2)}) collective-permute-start(f32[128,1024]{1,0:T(8,128)S(1)} %broadcast_select_fusion.3.refs_0_), channel_id=1, source_target_pairs={{4,0},{5,1},{6,2},{7,3},{8,12},{9,13},{10,14},{11,15},{20,16},{21,... | collective-permute-start | bytes 1572872 | tf_op jit(solution)/shard_map/ppermute | solution.py:338
  110.8 14.9 %collective-permute-start.14 = (f32[128,1024]{1,0:T(8,128)S(1)}, f32[128,1024]{1,0:T(8,128)}, u32[]{:S(2)}, u32[]{:S(2)}) collective-permute-start(f32[128,1024]{1,0:T(8,128)S(1)} %broadcast_select_fusion.2.refs_1_), channel_id=1, source_target_pairs={{0,2},{1,3},{2,0},{3,1},{4,6},{5,7},{6,4},{7,5},{8,10},{9,11},{10,... | collective-permute-start | bytes 1572872 | tf_op jit(solution)/shard_map/ppermute | solution.py:338
  117.6 18.6 %collective-permute-start.25 = (f32[128,1024]{1,0:T(8,128)S(1)}, f32[128,1024]{1,0:T(8,128)}, u32[]{:S(2)}, u32[]{:S(2)}) collective-permute-start(f32[128,1024]{1,0:T(8,128)S(1)} %broadcast_select_fusion.3.refs_0_), channel_id=1, source_target_pairs={{0,2},{1,3},{2,0},{3,1},{4,6},{5,7},{6,4},{7,5},{8,10},{9,11},{10,... | collective-permute-start | bytes 1572872 | tf_op jit(solution)/shard_map/ppermute | solution.py:338
  118.1 19.5 %collective-permute-start.22 = (f32[128,1024]{1,0:T(8,128)}, f32[128,1024]{1,0:T(8,128)S(1)}, u32[]{:S(2)}, u32[]{:S(2)}) collective-permute-start(f32[128,1024]{1,0:T(8,128)} %collective-permute-done.6.refs_1_), channel_id=1, source_target_pairs={{0,1},{1,0},{2,3},{3,2},{4,5},{5,4},{6,7},{7,6},{8,9},{9,8},{10,11... | collective-permute-start | bytes 1572872 | tf_op jit(solution)/shard_map/ppermute | solution.py:338
  128.7 17.6 %collective-permute-start.7 = (f32[128,1024]{1,0:T(8,128)}, f32[128,1024]{1,0:T(8,128)}, u32[]{:S(2)}, u32[]{:S(2)}) collective-permute-start(f32[128,1024]{1,0:T(8,128)} %collective-permute-done.6.refs_1_), channel_id=1, source_target_pairs={{0,2},{1,3},{2,0},{3,1},{12,14},{13,15},{14,12},{15,13},{16,18},{1... | collective-permute-start | bytes 1572872 | tf_op jit(solution)/shard_map/ppermute | solution.py:338
  138.5 29.0 %collective-permute-start.26 = (f32[128,1024]{1,0:T(8,128)}, f32[128,1024]{1,0:T(8,128)}, u32[]{:S(2)}, u32[]{:S(2)}) collective-permute-start(f32[128,1024]{1,0:T(8,128)} %collective-permute-done.25.refs_8_), channel_id=1, source_target_pairs={{0,1},{1,0},{2,3},{3,2},{4,5},{5,4},{6,7},{7,6},{8,9},{9,8},{10,11... | collective-permute-start | bytes 1572872 | tf_op jit(solution)/shard_map/ppermute | solution.py:338
  138.7 33.7 %collective-permute-start.16 = (f32[128,1024]{1,0:T(8,128)S(1)}, f32[128,1024]{1,0:T(8,128)S(1)}, u32[]{:S(2)}, u32[]{:S(2)}) collective-permute-start(f32[128,1024]{1,0:T(8,128)S(1)} %collective-permute-done.1.refs_0_), channel_id=1, source_target_pairs={{0,1},{1,0},{2,3},{3,2},{4,5},{5,4},{6,7},{7,6},{8,9},{9,8},{10,11... | collective-permute-start | bytes 1572872 | tf_op jit(solution)/shard_map/ppermute | solution.py:338
  139.3 33.2 %collective-permute-start.18 = (f32[128,1024]{1,0:T(8,128)S(1)}, f32[128,1024]{1,0:T(8,128)S(1)}, u32[]{:S(2)}, u32[]{:S(2)}) collective-permute-start(f32[128,1024]{1,0:T(8,128)S(1)} %collective-permute-done.9.refs_2_), channel_id=1, source_target_pairs={{0,1},{1,0},{2,3},{3,2},{4,5},{5,4},{6,7},{7,6},{8,9},{9,8},{10,11... | collective-permute-start | bytes 1572872 | tf_op jit(solution)/shard_map/ppermute | solution.py:338
  146.3 26.2 %collective-permute-start.17 = (f32[128,1024]{1,0:T(8,128)}, f32[128,1024]{1,0:T(8,128)S(1)}, u32[]{:S(2)}, u32[]{:S(2)}) collective-permute-start(f32[128,1024]{1,0:T(8,128)} %collective-permute-done.7.refs_1_), channel_id=1, source_target_pairs={{0,1},{1,0},{2,3},{3,2},{4,5},{5,4},{6,7},{7,6},{8,9},{9,8},{10,11... | collective-permute-start | bytes 1572872 | tf_op jit(solution)/shard_map/ppermute | solution.py:338
  149.6 23.0 %collective-permute-start.19 = (f32[128,1024]{1,0:T(8,128)}, f32[128,1024]{1,0:T(8,128)S(1)}, u32[]{:S(2)}, u32[]{:S(2)}) collective-permute-start(f32[128,1024]{1,0:T(8,128)} %collective-permute-done.15.refs_3_), channel_id=1, source_target_pairs={{0,1},{1,0},{2,3},{3,2},{4,5},{5,4},{6,7},{7,6},{8,9},{9,8},{10,11... | collective-permute-start | bytes 1572872 | tf_op jit(solution)/shard_map/ppermute | solution.py:338
  (56 other events, 766.0 us)
where the time goes:
time: 182 us; the launch traced here: 181 us
  waiting for transfers between devices  106 us (58%)
  starting transfers between devices  27.1 us (15%)
  Pallas kernels  23.3 us (13%)
  local copies, waits for them, and re-layouts  22.5 us (12%)
  between operations  1.87 us (1%)
    ppermute x40, waiting for transfers between devices, send(): return lax.ppermute(x, 'cluster', pairs)  106 us
    ppermute x40, starting transfers between devices, send(): return lax.ppermute(x, 'cluster', pairs)  27.1 us
    unnamed x82, local copies, waits for them, and re-layouts  19.9 us
    pallas_call x3, Pallas kernels, step_call(): pl.pallas_call(functools.partial(step_kernel, tuple((len(s) for s in slot...  14.4 us
    pallas_call x1, Pallas kernels, last_call(): pl.pallas_call(functools.partial(last_kernel, tuple((len(s) for s in slot...  8.89 us
  transfers between devices with their start and end apart: 40, of which 11 were waited for; matrix products, arithmetic and copies ran while one was open for 1% of the time, Pallas kernels for 8%

commit v1 on v0

--- a/solution.py
+++ b/solution.py
@@ -179,7 +179,7 @@
 
 def columns_of(ref, width):
     return [
-        jnp.broadcast_to(ref[:, j : j + 1], (ref.shape[0], width)) for j in range(ref.shape[1])
+        jnp.broadcast_to(ref[j : j + 1, :], (width, ref.shape[1])).T for j in range(ref.shape[0])
     ]
 
 
@@ -235,9 +235,9 @@
     expanded = queries + coefficient * (vector / total)
     expanded_ref[...] = expanded
     asked = stacked_halves(expanded)
-    per_query = ub_ref.shape[1]
-    for j in range(per_query):
-        named_ref[j] = jnp.broadcast_to(ub_ref[:, j : j + 1], (ub_ref.shape[0], rows))
+    per_query = ub_ref.shape[0]
+    for j, column in enumerate(columns_of(ub_ref, rows)):
+        named_ref[j] = column
     picked = [jnp.zeros((queries.shape[0], rows), jnp.float32) for _ in range(per_query)]
     for start, count, high, low in kept:
         scores = three_way(asked, high[...], low[...], NT)
@@ -288,7 +288,7 @@
     block = slots[0][0]
     count, rows, width = len(slots), block.shape[0], block.shape[1]
     flat = [ref for slot in slots for ref in slot]
-    many, per_query = followup_blocks.shape
+    per_query, many = followup_blocks.shape
     kept = [a for _, _, high, low in held for a in (high, low)]
     total = count + sum(n for _, n, _, _ in held)
     return pl.pallas_call(
@@ -395,7 +395,7 @@
         pairs, blocks = first_blocks.size, owners * resident
         capacity = max(2, (3 * pairs + 2 * blocks - 1) // (2 * blocks))
         if ladder is not None and blocks * rows <= 2 * 3 * blocks * capacity:
-            return gathered(ladder, queries, passages, first_blocks, followup_blocks)
+            return gathered(ladder, queries, passages, first_blocks.T, followup_blocks.T)
         return routed(queries, passages, first_blocks, followup_blocks)
 
     return jax.shard_map(

time: 182 us -> 171 us (0.940)
  local copies, waits for them, and re-layouts: 22.5 us -> 4.16 us
  waiting for transfers between devices: 106 us -> 116 us
  Pallas kernels: 23.3 us -> 21.1 us
    unnamed x82 -> x14, local copies, waits for them, and re-layouts: 19.9 us -> 1.61 us
    ppermute x40, waiting for transfers between devices: 106 us -> 116 us  [send(): return lax.ppermute(x, 'cluster', pairs)]
  transfers between devices with their start and end apart: 40 -> 40, of which waited for: 11 -> 13; matrix products, arithmetic and copies ran while one was open for 1% -> 1% of each run, Pallas kernels for 8% -> 8%
where the time goes in v1:
time: 171 us; the launch traced here: 170 us
  waiting for transfers between devices  116 us (68%)
  starting transfers between devices  27.3 us (16%)
  Pallas kernels  21.1 us (12%)
  local copies, waits for them, and re-layouts  4.16 us (2%)
    ppermute x40, waiting for transfers between devices, send(): return lax.ppermute(x, 'cluster', pairs)  116 us
    ppermute x40, starting transfers between devices, send(): return lax.ppermute(x, 'cluster', pairs)  27.3 us
    pallas_call x3, Pallas kernels, step_call(): pl.pallas_call(functools.partial(step_kernel, tuple((len(s) for s in slot...  12.9 us
    pallas_call x1, Pallas kernels, last_call(): pl.pallas_call(functools.partial(last_kernel, tuple((len(s) for s in slot...  8.26 us
  transfers between devices with their start and end apart: 40, of which 13 were waited for; matrix products, arithmetic and copies ran while one was open for 1% of the time, Pallas kernels for 8%

profile of v1, /device:TPU:0, one launch (start us, length us, event | category | flops | bytes accessed | tf_op | source)
XLA Modules:
  0.0 170.3 jit_solution(6960932614656519116)
XLA Ops:
  1.9 3.1 %collective-permute-start.2 = (f32[128,1024]{1,0:T(8,128)S(1)}, f32[128,1024]{1,0:T(8,128)S(1)}, u32[]{:S(2)}, u32[]{:S(2)}) collective-permute-start(f32[128,1024]{1,0:T(8,128)S(1)} %get-tuple-element.27.refs_0_), channel_id=1, source_target_pairs={{0,4},{1,5},{2,6},{3,7},{4,0},{5,1},{6,2},{7,3},{8,12},{9,13},{10,... | collective-permute-start | bytes 1572872 | tf_op jit(solution)/shard_map/ppermute | solution.py:338
  5.1 1.9 %collective-permute-start = (f32[128,1024]{1,0:T(8,128)S(1)}, f32[128,1024]{1,0:T(8,128)}, u32[]{:S(2)}, u32[]{:S(2)}) collective-permute-start(f32[128,1024]{1,0:T(8,128)S(1)} %get-tuple-element.27.refs_0_), channel_id=1, source_target_pairs={{0,2},{1,3},{2,0},{3,1},{4,6},{5,7},{6,4},{7,5},{8,10},{9,11},{10,... | collective-permute-start | bytes 1572872 | tf_op jit(solution)/shard_map/ppermute | solution.py:338
  7.1 10.7 %collective-permute-done.2.refs_4_ = f32[128,1024]{1,0:T(8,128)S(1)} collective-permute-done((f32[128,1024]{1,0:T(8,128)S(1)}, f32[128,1024]{1,0:T(8,128)S(1)}, u32[]{:S(2)}, u32[]{:S(2)}) %collective-permute-start.2) | collective-permute-done | bytes 524320 | tf_op jit(solution)/shard_map/ppermute | solution.py:338
  17.8 10.4 %collective-permute-done.10.refs_5_ = f32[128,1024]{1,0:T(8,128)S(1)} collective-permute-done((f32[128,1024]{1,0:T(8,128)S(1)}, f32[128,1024]{1,0:T(8,128)S(1)}, u32[]{:S(2)}, u32[]{:S(2)}) %collective-permute-start.10) | collective-permute-done | bytes 524320 | tf_op jit(solution)/shard_map/ppermute | solution.py:338
  37.3 1.4 collective-permute-start.13
  38.8 1.7 collective-permute-start.30
  40.9 34.6 %collective-permute-done.5 = f32[128,1024]{1,0:T(8,128)S(1)} collective-permute-done((f32[128,1024]{1,0:T(8,128)S(1)}, f32[128,1024]{1,0:T(8,128)S(1)}, u32[]{:S(2)}, u32[]{:S(2)}) %collective-permute-start.5) | collective-permute-done | bytes 524320 | tf_op jit(solution)/shard_map/ppermute | solution.py:338
  76.0 10.4 %collective-permute-done.13 = f32[128,1024]{1,0:T(8,128)S(1)} collective-permute-done((f32[128,1024]{1,0:T(8,128)S(1)}, f32[128,1024]{1,0:T(8,128)S(1)}, u32[]{:S(2)}, u32[]{:S(2)}) %collective-permute-start.13) | collective-permute-done | bytes 524320 | tf_op jit(solution)/shard_map/ppermute | solution.py:338
  86.5 1.5 collective-permute-start.1
  88.0 1.3 collective-permute-start.9
  90.1 10.5 %collective-permute-done.1.refs_0_ = f32[128,1024]{1,0:T(8,128)S(1)} collective-permute-done((f32[128,1024]{1,0:T(8,128)}, f32[128,1024]{1,0:T(8,128)S(1)}, u32[]{:S(2)}, u32[]{:S(2)}) %collective-permute-start.1) | collective-permute-done | bytes 524320 | tf_op jit(solution)/shard_map/ppermute | solution.py:338
  101.8 9.0 %collective-permute-done.9.refs_2_ = f32[128,1024]{1,0:T(8,128)S(1)} collective-permute-done((f32[128,1024]{1,0:T(8,128)}, f32[128,1024]{1,0:T(8,128)S(1)}, u32[]{:S(2)}, u32[]{:S(2)}) %collective-permute-start.9) | collective-permute-done | bytes 524320 | tf_op jit(solution)/shard_map/ppermute | solution.py:338
  110.8 1.5 collective-permute-start.14
  114.5 11.1 %collective-permute-done.14.refs_9_ = f32[128,1024]{1,0:T(8,128)S(1)} collective-permute-done((f32[128,1024]{1,0:T(8,128)S(1)}, f32[128,1024]{1,0:T(8,128)S(1)}, u32[]{:S(2)}, u32[]{:S(2)}) %collective-permute-start.14) | collective-permute-done | bytes 524320 | tf_op jit(solution)/shard_map/ppermute | solution.py:338
  125.6 1.3 collective-permute-done.20.refs_3_
  127.0 2.6 %collective-permute-start.7 = (f32[128,1024]{1,0:T(8,128)S(1)}, f32[128,1024]{1,0:T(8,128)S(1)}, u32[]{:S(2)}, u32[]{:S(2)}) collective-permute-start(f32[128,1024]{1,0:T(8,128)S(1)} %collective-permute-done.6.refs_1_), channel_id=1, source_target_pairs={{0,2},{1,3},{2,0},{3,1},{12,14},{13,15},{14,12},{15,13},{16,18},{1... | collective-permute-start | bytes 1572872 | tf_op jit(solution)/shard_map/ppermute | solution.py:338
  129.6 7.3 %collective-permute-done.25.refs_8_ = f32[128,1024]{1,0:T(8,128)S(1)} collective-permute-done((f32[128,1024]{1,0:T(8,128)S(1)}, f32[128,1024]{1,0:T(8,128)S(1)}, u32[]{:S(2)}, u32[]{:S(2)}) %collective-permute-start.25) | collective-permute-done | bytes 524320 | tf_op jit(solution)/shard_map/ppermute | solution.py:338
  136.9 1.5 collective-permute-start.15
  139.0 7.3 %collective-permute-done.7.refs_1_ = f32[128,1024]{1,0:T(8,128)S(1)} collective-permute-done((f32[128,1024]{1,0:T(8,128)S(1)}, f32[128,1024]{1,0:T(8,128)S(1)}, u32[]{:S(2)}, u32[]{:S(2)}) %collective-permute-start.7) | collective-permute-done | bytes 524320 | tf_op jit(solution)/shard_map/ppermute | solution.py:338
  146.3 2.8 %collective-permute-done.15.refs_3_ = f32[128,1024]{1,0:T(8,128)S(1)} collective-permute-done((f32[128,1024]{1,0:T(8,128)S(1)}, f32[128,1024]{1,0:T(8,128)S(1)}, u32[]{:S(2)}, u32[]{:S(2)}) %collective-permute-start.15) | collective-permute-done | bytes 524320 | tf_op jit(solution)/shard_map/ppermute | solution.py:338
  149.1 5.8 %first_round_step.3 = (f32[128,128]{1,0:T(8,128)S(1)}, f32[128,1024]{1,0:T(8,128)S(1)}, bf16[1536,1024]{1,0:T(8,128)(2,1)S(1)}, bf16[1536,1024]{1,0:T(8,128)(2,1)S(1)}) custom-call(s32[33]{0:T(128)S(1)} %get-tuple-element.29.ids, f32[128,1024]{1,0:T(8,128)S(1)} %get-tuple-element.27.refs_0_, f32[128,1024]{1,0:T(8,128)S(1)} %get-tuple-element.26.refs_1_, ...), custom_call_target="tpu_custom_call" | custom-call | flops 2415919104 | bytes 6291456 | tf_op jit(solution)/shard_map/first_round_step/pallas_call | solution.py:270
  154.9 3.5 %first_round_step.4 = (f32[128,128]{1,0:T(8,128)S(1)}, f32[128,1024]{1,0:T(8,128)S(1)}, bf16[1024,1024]{1,0:T(8,128)(2,1)S(1)}, bf16[1024,1024]{1,0:T(8,128)(2,1)S(1)}) custom-call(s32[33]{0:T(128)S(1)} %get-tuple-element.29.ids, f32[128,1024]{1,0:T(8,128)S(1)} %broadcast_select_fusion.3.refs_0_, f32[128,1024]{1,0:T(8,128)S(1)} %broadcast_select_fusion.2.refs_1_, ...), custom_call_target="tpu_custom_call" | custom-call | flops 1610612736 | bytes 4194304 | tf_op jit(solution)/shard_map/first_round_step/pallas_call | solution.py:270
  158.5 3.5 %first_round_step.5 = (f32[128,128]{1,0:T(8,128)S(1)}, f32[128,1024]{1,0:T(8,128)S(1)}, bf16[1024,1024]{1,0:T(8,128)(2,1)S(1)}, bf16[1024,1024]{1,0:T(8,128)(2,1)S(1)}) custom-call(s32[33]{0:T(128)S(1)} %get-tuple-element.29.ids, f32[128,1024]{1,0:T(8,128)S(1)} %collective-permute-done.4.refs_0_, f32[128,1024]{1,0:T(8,128)S(1)} %collective-permute-done.6.refs_1_, ...), custom_call_target="tpu_custom_call" | custom-call | flops 1610612736 | bytes 4194304 | tf_op jit(solution)/shard_map/first_round_step/pallas_call | solution.py:270
  162.1 8.3 %second_round.1 = (f32[128,1024]{1,0:T(8,128)}, f32[128,4,128]{2,1,0:T(4,128)}) custom-call(s32[33]{0:T(128)S(1)} %get-tuple-element.29.ids, f32[128,1024]{1,0:T(8,128)S(1)} %collective-permute-done.1.refs_0_, f32[128,1024]{1,0:T(8,128)S(1)} %collective-permute-done.7.refs_1_, f32[128,1024]{1,0:T(8,128)S(1)} %collective-permute-done.9.refs_2_, ...), custom_call_target="tpu_custom_call" | custom-call | flops 3221225472 | bytes 16777216 | tf_op jit(solution)/shard_map/second_round/pallas_call | solution.py:294
  (81 shorter events, 15.7 us)
Async XLA Ops:
  1.9 15.9 %collective-permute-start.2 = (f32[128,1024]{1,0:T(8,128)S(1)}, f32[128,1024]{1,0:T(8,128)S(1)}, u32[]{:S(2)}, u32[]{:S(2)}) collective-permute-start(f32[128,1024]{1,0:T(8,128)S(1)} %get-tuple-element.27.refs_0_), channel_id=1, source_target_pairs={{0,4},{1,5},{2,6},{3,7},{4,0},{5,1},{6,2},{7,3},{8,12},{9,13},{10,... | collective-permute-start | bytes 1572872 | tf_op jit(solution)/shard_map/ppermute | solution.py:338
  5.0 23.2 %collective-permute-start.10 = (f32[128,1024]{1,0:T(8,128)S(1)}, f32[128,1024]{1,0:T(8,128)S(1)}, u32[]{:S(2)}, u32[]{:S(2)}) collective-permute-start(f32[128,1024]{1,0:T(8,128)S(1)} %get-tuple-element.26.refs_1_), channel_id=1, source_target_pairs={{0,4},{1,5},{2,6},{3,7},{4,0},{5,1},{6,2},{7,3},{8,12},{9,13},{10,... | collective-permute-start | bytes 1572872 | tf_op jit(solution)/shard_map/ppermute | solution.py:338
  5.1 23.8 %collective-permute-start = (f32[128,1024]{1,0:T(8,128)S(1)}, f32[128,1024]{1,0:T(8,128)}, u32[]{:S(2)}, u32[]{:S(2)}) collective-permute-start(f32[128,1024]{1,0:T(8,128)S(1)} %get-tuple-element.27.refs_0_), channel_id=1, source_target_pairs={{0,2},{1,3},{2,0},{3,1},{4,6},{5,7},{6,4},{7,5},{8,10},{9,11},{10,... | collective-permute-start | bytes 1572872 | tf_op jit(solution)/shard_map/ppermute | solution.py:338
  7.0 22.8 %collective-permute-start.8 = (f32[128,1024]{1,0:T(8,128)S(1)}, f32[128,1024]{1,0:T(8,128)}, u32[]{:S(2)}, u32[]{:S(2)}) collective-permute-start(f32[128,1024]{1,0:T(8,128)S(1)} %get-tuple-element.26.refs_1_), channel_id=1, source_target_pairs={{0,2},{1,3},{2,0},{3,1},{4,6},{5,7},{6,4},{7,5},{8,10},{9,11},{10,... | collective-permute-start | bytes 1572872 | tf_op jit(solution)/shard_map/ppermute | solution.py:338
  7.1 22.7 %collective-permute-start.34 = (f32[128,1024]{1,0:T(8,128)S(1)}, f32[128,1024]{1,0:T(8,128)S(1)}, u32[]{:S(2)}, u32[]{:S(2)}) collective-permute-start(f32[128,1024]{1,0:T(8,128)S(1)} %get-tuple-element.27.refs_0_), channel_id=1, source_target_pairs={{0,1},{1,0},{2,3},{3,2},{4,5},{5,4},{6,7},{7,6},{8,9},{9,8},{10,11... | collective-permute-start | bytes 1572872 | tf_op jit(solution)/shard_map/ppermute | solution.py:338
  34.6 40.9 %collective-permute-start.11 = (f32[128,1024]{1,0:T(8,128)S(1)}, f32[128,1024]{1,0:T(8,128)S(1)}, u32[]{:S(2)}, u32[]{:S(2)}) collective-permute-start(f32[128,1024]{1,0:T(8,128)S(1)} %collective-permute-done.10.refs_5_), channel_id=1, source_target_pairs={{4,8},{5,9},{6,10},{7,11},{8,4},{9,5},{10,6},{11,7},{20,24},{21,25... | collective-permute-start | bytes 1572872 | tf_op jit(solution)/shard_map/ppermute | solution.py:338
  35.9 39.6 %collective-permute-start.5 = (f32[128,1024]{1,0:T(8,128)S(1)}, f32[128,1024]{1,0:T(8,128)S(1)}, u32[]{:S(2)}, u32[]{:S(2)}) collective-permute-start(f32[128,1024]{1,0:T(8,128)S(1)} %collective-permute-done.4.refs_0_), channel_id=1, source_target_pairs={{4,0},{5,1},{6,2},{7,3},{8,12},{9,13},{10,14},{11,15},{20,16},{21,... | collective-permute-start | bytes 1572872 | tf_op jit(solution)/shard_map/ppermute | solution.py:338
  37.3 49.2 %collective-permute-start.13 = (f32[128,1024]{1,0:T(8,128)S(1)}, f32[128,1024]{1,0:T(8,128)S(1)}, u32[]{:S(2)}, u32[]{:S(2)}) collective-permute-start(f32[128,1024]{1,0:T(8,128)S(1)} %collective-permute-done.12.refs_2_), channel_id=1, source_target_pairs={{4,0},{5,1},{6,2},{7,3},{8,12},{9,13},{10,14},{11,15},{20,16},{21,... | collective-permute-start | bytes 1572872 | tf_op jit(solution)/shard_map/ppermute | solution.py:338
  38.8 49.2 %collective-permute-start.30 = (f32[128,1024]{1,0:T(8,128)S(1)}, f32[128,1024]{1,0:T(8,128)S(1)}, u32[]{:S(2)}, u32[]{:S(2)}) collective-permute-start(f32[128,1024]{1,0:T(8,128)S(1)} %broadcast_select_fusion.1), channel_id=1, source_target_pairs={{0,2},{1,3},{2,0},{3,1},{4,6},{5,7},{6,4},{7,5},{8,10},{9,11},{10,... | collective-permute-start | bytes 1572872 | tf_op jit(solution)/shard_map/ppermute | solution.py:338
  40.5 48.9 %collective-permute-start.31 = (f32[128,1024]{1,0:T(8,128)S(1)}, f32[128,1024]{1,0:T(8,128)S(1)}, u32[]{:S(2)}, u32[]{:S(2)}) collective-permute-start(f32[128,1024]{1,0:T(8,128)S(1)} %broadcast_select_fusion), channel_id=1, source_target_pairs={{0,2},{1,3},{2,0},{3,1},{4,6},{5,7},{6,4},{7,5},{8,10},{9,11},{10,... | collective-permute-start | bytes 1572872 | tf_op jit(solution)/shard_map/ppermute | solution.py:338
  75.5 14.5 %collective-permute-start.23 = (f32[128,1024]{1,0:T(8,128)S(1)}, f32[128,1024]{1,0:T(8,128)S(1)}, u32[]{:S(2)}, u32[]{:S(2)}) collective-permute-start(f32[128,1024]{1,0:T(8,128)S(1)} %collective-permute-done.12.refs_2_), channel_id=1, source_target_pairs={{0,1},{1,0},{2,3},{3,2},{4,5},{5,4},{6,7},{7,6},{8,9},{9,8},{10,11... | collective-permute-start | bytes 1572872 | tf_op jit(solution)/shard_map/ppermute | solution.py:338
  88.0 22.8 %collective-permute-start.9 = (f32[128,1024]{1,0:T(8,128)}, f32[128,1024]{1,0:T(8,128)S(1)}, u32[]{:S(2)}, u32[]{:S(2)}) collective-permute-start(f32[128,1024]{1,0:T(8,128)} %collective-permute-done.8.refs_9_), channel_id=1, source_target_pairs={{0,4},{1,5},{2,6},{3,7},{12,8},{13,9},{14,10},{15,11},{16,20},{17,... | collective-permute-start | bytes 1572872 | tf_op jit(solution)/shard_map/ppermute | solution.py:338
  89.4 23.0 %collective-permute-start.28 = (f32[128,1024]{1,0:T(8,128)S(1)}, f32[128,1024]{1,0:T(8,128)S(1)}, u32[]{:S(2)}, u32[]{:S(2)}) collective-permute-start(f32[128,1024]{1,0:T(8,128)S(1)} %broadcast_select_fusion.3.refs_0_), channel_id=1, source_target_pairs={{0,1},{1,0},{2,3},{3,2},{4,5},{5,4},{6,7},{7,6},{8,9},{9,8},{10,11... | collective-permute-start | bytes 1572872 | tf_op jit(solution)/shard_map/ppermute | solution.py:338
  89.5 24.2 %collective-permute-start.29 = (f32[128,1024]{1,0:T(8,128)S(1)}, f32[128,1024]{1,0:T(8,128)S(1)}, u32[]{:S(2)}, u32[]{:S(2)}) collective-permute-start(f32[128,1024]{1,0:T(8,128)S(1)} %broadcast_select_fusion.2.refs_1_), channel_id=1, source_target_pairs={{0,1},{1,0},{2,3},{3,2},{4,5},{5,4},{6,7},{7,6},{8,9},{9,8},{10,11... | collective-permute-start | bytes 1572872 | tf_op jit(solution)/shard_map/ppermute | solution.py:338
  90.0 23.8 %collective-permute-start.32 = (f32[128,1024]{1,0:T(8,128)S(1)}, f32[128,1024]{1,0:T(8,128)S(1)}, u32[]{:S(2)}, u32[]{:S(2)}) collective-permute-start(f32[128,1024]{1,0:T(8,128)S(1)} %collective-permute-done.30.refs_4_), channel_id=1, source_target_pairs={{0,1},{1,0},{2,3},{3,2},{4,5},{5,4},{6,7},{7,6},{8,9},{9,8},{10,11... | collective-permute-start | bytes 1572872 | tf_op jit(solution)/shard_map/ppermute | solution.py:338
  110.8 14.8 %collective-permute-start.14 = (f32[128,1024]{1,0:T(8,128)S(1)}, f32[128,1024]{1,0:T(8,128)S(1)}, u32[]{:S(2)}, u32[]{:S(2)}) collective-permute-start(f32[128,1024]{1,0:T(8,128)S(1)} %broadcast_select_fusion.2.refs_1_), channel_id=1, source_target_pairs={{0,2},{1,3},{2,0},{3,1},{4,6},{5,7},{6,4},{7,5},{8,10},{9,11},{10,... | collective-permute-start | bytes 1572872 | tf_op jit(solution)/shard_map/ppermute | solution.py:338
  112.4 14.6 %collective-permute-start.20 = (f32[128,1024]{1,0:T(8,128)S(1)}, f32[128,1024]{1,0:T(8,128)S(1)}, u32[]{:S(2)}, u32[]{:S(2)}) collective-permute-start(f32[128,1024]{1,0:T(8,128)S(1)} %broadcast_select_fusion.2.refs_1_), channel_id=1, source_target_pairs={{4,0},{5,1},{6,2},{7,3},{8,12},{9,13},{10,14},{11,15},{20,16},{21,... | collective-permute-start | bytes 1572872 | tf_op jit(solution)/shard_map/ppermute | solution.py:338
  113.8 23.1 %collective-permute-start.25 = (f32[128,1024]{1,0:T(8,128)S(1)}, f32[128,1024]{1,0:T(8,128)S(1)}, u32[]{:S(2)}, u32[]{:S(2)}) collective-permute-start(f32[128,1024]{1,0:T(8,128)S(1)} %broadcast_select_fusion.3.refs_0_), channel_id=1, source_target_pairs={{0,2},{1,3},{2,0},{3,1},{4,6},{5,7},{6,4},{7,5},{8,10},{9,11},{10,... | collective-permute-start | bytes 1572872 | tf_op jit(solution)/shard_map/ppermute | solution.py:338
  114.5 23.8 %collective-permute-start.22 = (f32[128,1024]{1,0:T(8,128)S(1)}, f32[128,1024]{1,0:T(8,128)S(1)}, u32[]{:S(2)}, u32[]{:S(2)}) collective-permute-start(f32[128,1024]{1,0:T(8,128)S(1)} %collective-permute-done.6.refs_1_), channel_id=1, source_target_pairs={{0,1},{1,0},{2,3},{3,2},{4,5},{5,4},{6,7},{7,6},{8,9},{9,8},{10,11... | collective-permute-start | bytes 1572872 | tf_op jit(solution)/shard_map/ppermute | solution.py:338
  127.0 19.3 %collective-permute-start.7 = (f32[128,1024]{1,0:T(8,128)S(1)}, f32[128,1024]{1,0:T(8,128)S(1)}, u32[]{:S(2)}, u32[]{:S(2)}) collective-permute-start(f32[128,1024]{1,0:T(8,128)S(1)} %collective-permute-done.6.refs_1_), channel_id=1, source_target_pairs={{0,2},{1,3},{2,0},{3,1},{12,14},{13,15},{14,12},{15,13},{16,18},{1... | collective-permute-start | bytes 1572872 | tf_op jit(solution)/shard_map/ppermute | solution.py:338
  138.3 20.1 %collective-permute-start.26 = (f32[128,1024]{1,0:T(8,128)S(1)}, f32[128,1024]{1,0:T(8,128)S(1)}, u32[]{:S(2)}, u32[]{:S(2)}) collective-permute-start(f32[128,1024]{1,0:T(8,128)S(1)} %collective-permute-done.25.refs_8_), channel_id=1, source_target_pairs={{0,1},{1,0},{2,3},{3,2},{4,5},{5,4},{6,7},{7,6},{8,9},{9,8},{10,11... | collective-permute-start | bytes 1572872 | tf_op jit(solution)/shard_map/ppermute | solution.py:338
  138.4 23.6 %collective-permute-start.16 = (f32[128,1024]{1,0:T(8,128)S(1)}, f32[128,1024]{1,0:T(8,128)S(1)}, u32[]{:S(2)}, u32[]{:S(2)}) collective-permute-start(f32[128,1024]{1,0:T(8,128)S(1)} %collective-permute-done.1.refs_0_), channel_id=1, source_target_pairs={{0,1},{1,0},{2,3},{3,2},{4,5},{5,4},{6,7},{7,6},{8,9},{9,8},{10,11... | collective-permute-start | bytes 1572872 | tf_op jit(solution)/shard_map/ppermute | solution.py:338
  138.9 23.1 %collective-permute-start.18 = (f32[128,1024]{1,0:T(8,128)S(1)}, f32[128,1024]{1,0:T(8,128)S(1)}, u32[]{:S(2)}, u32[]{:S(2)}) collective-permute-start(f32[128,1024]{1,0:T(8,128)S(1)} %collective-permute-done.9.refs_2_), channel_id=1, source_target_pairs={{0,1},{1,0},{2,3},{3,2},{4,5},{5,4},{6,7},{7,6},{8,9},{9,8},{10,11... | collective-permute-start | bytes 1572872 | tf_op jit(solution)/shard_map/ppermute | solution.py:338
  146.3 15.8 %collective-permute-start.17 = (f32[128,1024]{1,0:T(8,128)S(1)}, f32[128,1024]{1,0:T(8,128)S(1)}, u32[]{:S(2)}, u32[]{:S(2)}) collective-permute-start(f32[128,1024]{1,0:T(8,128)S(1)} %collective-permute-done.7.refs_1_), channel_id=1, source_target_pairs={{0,1},{1,0},{2,3},{3,2},{4,5},{5,4},{6,7},{7,6},{8,9},{9,8},{10,11... | collective-permute-start | bytes 1572872 | tf_op jit(solution)/shard_map/ppermute | solution.py:338
  (23 other events, 608.9 us)
